TPU v7x, 256 devices: a whole 4x4x8 slice. The times are simulated.
256 devices in a mesh: pair: 16 (over z, core), red: 16 (over x, y).
Axes of the slice: x: 4, y: 4, z: 8, core: 2. Of those that a mesh axis runs over, the one named last changes fastest.
Arguments:
- three_center: bfloat16 [2304, 256, 256], P('pair', 'red'), may hold values from -0.375 to 0.375
- occ_src: int32 [256, 16], P('red'), may hold values from 0 to 15, as said below
- occ_block: int32 [256, 16], P('red'), may hold values from 0 to 31
- occ_blocks: bfloat16 [512, 256], P('red'), may hold values from -0.375 to 0.375
- virt_block: int32 [16, 16, 1], P('red'), may hold values from 0 to 31, as said below
- virt_blocks: bfloat16 [16, 32, 256], P('red', 'pair'), may hold values from -1.5 to 1.5
Outputs:
- chi: float32 [2304, 2304], P('pair', 'red')
Inputs may be any that keep to these rules, and one draw needn't show every extreme that they name: `occ_src`: the 16 entries of a row are distinct. `virt_block`: every block listed for tile t of a red group lies from (t) * 2 to (t) * 2 + 1.
All inputs are finite; a program needn't handle non-finite values.
Results may differ from a plain program's by a relative error of at most 0.0041.
Values may be sent and summed in bfloat16 or wider, within the bound.
A program may use at most 128 MiB of HBM per device.

v0:
```python
import jax
import jax.numpy as jnp
from jax import lax
from jax.sharding import PartitionSpec as P

BLK = 16
TPD = 1


def occupied(three_center, occ_src, occ_block, occ_blocks):
    aux_rows, ntiles, area = three_center.shape
    nblocks = occ_blocks.shape[0]
    block_hot = (
        occ_block[:, :, None] == jnp.arange(nblocks, dtype=jnp.int32)[None, None, :]
    ).astype(jnp.bfloat16)
    picked = jnp.einsum(
        "tsb,bk->tsk", block_hot, occ_blocks, preferred_element_type=jnp.float32
    ).astype(jnp.bfloat16)
    source_hot = (occ_src[:, :, None] == jnp.arange(ntiles, dtype=jnp.int32)[None, None, :]).astype(
        jnp.bfloat16
    )
    mixing = jnp.einsum(
        "tsk,tsa->tka", source_hot, picked, preferred_element_type=jnp.float32
    ).astype(jnp.bfloat16)
    mixing = mixing.reshape(ntiles, ntiles, BLK, BLK)
    blocks = three_center.reshape(aux_rows, ntiles, BLK, BLK)
    half = jnp.einsum("tkml,pkln->ptmn", mixing, blocks, preferred_element_type=jnp.float32)
    return half.reshape(aux_rows, ntiles, area).astype(jnp.bfloat16)


def virtual(half, listed, blocks):
    aux_rows, ntiles, area = half.shape
    owners = listed.shape[0]
    nblocks = blocks.shape[0]
    block_hot = (listed[..., None] == jnp.arange(nblocks, dtype=jnp.int32)).astype(jnp.bfloat16)
    picked = jnp.einsum(
        "oijb,bk->oijk", block_hot, blocks, preferred_element_type=jnp.float32
    ).astype(jnp.bfloat16)
    picked = picked.reshape(owners, TPD, TPD, BLK, BLK)
    grouped = half.reshape(aux_rows, owners, TPD, BLK, BLK)
    kernel = jnp.einsum("pojml,oijln->poimn", grouped, picked, preferred_element_type=jnp.float32)
    return kernel.reshape(aux_rows, ntiles, area).astype(jnp.bfloat16)


def shards(three_center, occ_src, occ_block, occ_blocks, virt_block, virt_blocks):
    aux_rows, ntiles, area = three_center.shape
    half = occupied(three_center, occ_src, occ_block, occ_blocks)
    own_blocks = virt_blocks[0]
    listed = virt_block[0]
    all_blocks = lax.all_gather(own_blocks, "pair", axis=0, tiled=True)
    kernel = virtual(half, listed.reshape(ntiles // TPD, TPD, TPD), all_blocks)
    flat_tiles = three_center.reshape(aux_rows, ntiles * area)
    piece = lax.all_gather(kernel, "pair", axis=0, tiled=True)
    flat_piece = piece.reshape(piece.shape[0], ntiles * area)
    partial_value = lax.dot_general(
        flat_tiles, flat_piece, (((1,), (1,)), ((), ())), preferred_element_type=jnp.float32
    )
    return lax.psum_scatter(partial_value, "red", scatter_dimension=1, tiled=True)


def solution(mesh):
    placed = (
        P("pair", "red", None),
        P("red", None),
        P("red", None),
        P("red", None),
        P("red", None, None),
        P("red", "pair", None),
    )
    return jax.shard_map(
        shards, mesh=mesh, in_specs=placed, out_specs=P("pair", "red"), check_vma=False
    )
```

profile of v0, /device:TPU:32, one launch (start us, length us, event | category | flops | bytes accessed | tf_op | source)
XLA Modules:
  0.0 243.4 jit_solution(1345893647742258906)
XLA Ops:
  6.5 0.0 copy-start
  6.5 0.0 copy-start.1
  6.5 0.0 all-gather.3.cloned.1.call-start
  6.5 0.8 copy.21
  7.3 17.9 %all-gather = bf16[1,32,256]{2,0,1:T(2,128)(2,1)S(1)} all-gather(bf16[1,2,256]{2,0,1:T(2,128)(2,1)S(1)} %copy.21), channel_id=2, replica_groups=mesh['pair'=16,'red'=16] {'pair'}, dimensions={1}, use_global_device_ids=true | all-gather | bytes 17408 | tf_op jit(solution)/shard_map/all_gather | solution.py:50
  25.2 0.8 convolution_convert_fusion.2
  26.1 0.1 reshape.42
  26.2 0.0 copy-done
  26.2 1.1 convolution_convert_fusion
  27.3 1.7 reshape.47
  29.0 0.0 copy-done.1
  29.0 1.2 copy.22
  30.2 3.4 %fusion.7 = bf16[144,16,16,16]{0,2,3,1:T(8,128)(2,1)S(1)} fusion(bf16[144,16,16,16]{0,3,2,1:T(8,128)(2,1)S(1)} %bitcast.43, bf16[16,16,16,16,1]{3,2,1,0,4:T(8,128)(2,1)} %reshape.47), kind=kOutput, calls=%fused_computation.7 | convolution fusion | flops 302579712 | bytes 2490368 | tf_op jit(solution)/shard_map/tkml,pkln->ptmn/dot_general | solution.py:27
  33.5 2.2 fusion.4
  35.7 3.7 %copy.26 = bf16[144,16,256]{2,0,1:T(8,128)(2,1)} copy(bf16[144,16,256]{0,2,1:T(8,128)(2,1)} %bitcast.44) | data formatting | bytes 2359296 | tf_op jit(solution)/shard_map/convert_element_type | solution.py:42
  39.4 0.0 all-gather.3.cloned.1.call-update
  39.4 0.0 reduce-scatter.4.cloned.1.call-start
  39.5 103.4 %all-gather.3.cloned.1.call-done = bf16[2304,16,256]{2,0,1:T(8,128)(2,1)} async-done(((bf16[144,16,256]{2,0,1:T(8,128)(2,1)}), bf16[2304,16,256]{2,0,1:T(8,128)(2,1)}) %all-gather.3.cloned.1.call-update) | async-done | bytes 18874384 | tf_op jit(solution)/shard_map/all_gather | solution.py:53
  142.8 9.5 %convolution_bitcast_fusion = f32[144,2304]{1,0:T(8,128)S(1)} fusion(bf16[2304,16,256]{2,0,1:T(8,128)(2,1)} %all-gather.3.cloned.1.call-done, bf16[144,16,256]{0,2,1:T(8,128)(2,1)S(1)} %copy.22), kind=kOutput, calls=%fused_computation.1 | convolution fusion | flops 2717908992 | bytes 21381120 | tf_op jit(solution)/shard_map/dot_general | solution.py:55
  152.3 1.9 copy.33
  154.2 0.0 reduce-scatter.4.cloned.1.call-update
  154.3 80.6 %reduce-scatter.4.cloned.1.call-done = f32[144,144]{1,0:T(8,128)} async-done(((f32[2304,144]{1,0:T(8,128)}), f32[144,144]{1,0:T(8,128)}) %reduce-scatter.4.cloned.1.call-update) | async-done | bytes 82960
  234.9 1.7 copy.34
Async XLA Ops:
  6.5 19.6 %copy-start = (bf16[32,256]{1,0:T(8,128)(2,1)S(1)}, bf16[32,256]{1,0:T(8,128)(2,1)}, u32[]{:S(2)}) copy-start(bf16[32,256]{1,0:T(8,128)(2,1)} %param.9) | copy-start | bytes 49156
  6.5 22.4 %copy-start.1 = (bf16[144,16,256]{2,1,0:T(8,128)(2,1)S(1)}, bf16[144,16,256]{2,1,0:T(8,128)(2,1)}, u32[]{:S(2)}) copy-start(bf16[144,16,256]{2,1,0:T(8,128)(2,1)} %param.6) | copy-start | bytes 3538948
  6.5 136.3 %all-gather.3.cloned.1.call-start = ((), (), s32[]{:S(2)}) async-start(), calls=%async_computation.1 | async-start | bytes 20054016 | tf_op jit(solution)/shard_map/all_gather | solution.py:53
  39.4 195.4 %reduce-scatter.4.cloned.1.call-start = ((), (), s32[]{:S(2)}) async-start(), calls=%async_computation.2 | async-start | bytes 2506752
Sparse Core Ops, SparseCore 0:
  39.6 103.2 all-gather.2
  154.4 80.4 reduce-scatter.3
where the time goes:
time: 244 us; the launch traced here: 243 us
  waiting for transfers between devices  184 us (75%)
  blocking collectives  17.9 us (7%)
  matrix products  17 us (7%)
  between operations  13.4 us (5%)
  local copies, waits for them, and re-layouts  11 us (5%)
    all_gather x1, waiting for transfers between devices, shards(): piece = lax.all_gather(kernel, 'pair', axis=0, tiled=True)  103 us
    unnamed x3, waiting for transfers between devices  80.6 us
    all_gather x1, blocking collectives, shards(): all_blocks = lax.all_gather(own_blocks, 'pair', axis=0, tiled=True)  17.9 us
    dot_general x1, matrix products, shards(): lax.dot_general(flat_tiles, flat_piece, (((1,), (1,)), ((), ())), preferr...  9.48 us
    unnamed x8, local copies, waits for them, and re-layouts  5.55 us
  transfers between devices with their start and end apart: 2, of which 2 were waited for; matrix products, arithmetic and copies ran while one was open for 0% of the time, Pallas kernels for 0%

commit v1 on v0

--- a/solution.py
+++ b/solution.py
@@ -47,7 +47,23 @@
     half = occupied(three_center, occ_src, occ_block, occ_blocks)
     own_blocks = virt_blocks[0]
     listed = virt_block[0]
-    all_blocks = lax.all_gather(own_blocks, "pair", axis=0, tiled=True)
+    ways, here, turn = (lax.axis_size("pair"), lax.axis_index("pair"), own_blocks.shape[0])
+    dims = [n * ways if d == 0 else n for d, n in enumerate(own_blocks.shape)]
+    full = lax.dynamic_update_slice_in_dim(
+        jnp.zeros(dims, own_blocks.dtype), own_blocks, here * turn, axis=0
+    )
+    going_up = going_down = own_blocks
+    for far in range(1, ways // 2 + 1):
+        going_up = lax.ppermute(going_up, "pair", [(d, (d + 1) % ways) for d in range(ways)])
+        full = lax.dynamic_update_slice_in_dim(full, going_up, (here - far) % ways * turn, axis=0)
+        if 2 * far < ways:
+            going_down = lax.ppermute(
+                going_down, "pair", [(d, (d - 1) % ways) for d in range(ways)]
+            )
+            full = lax.dynamic_update_slice_in_dim(
+                full, going_down, (here + far) % ways * turn, axis=0
+            )
+    all_blocks = full
     kernel = virtual(half, listed.reshape(ntiles // TPD, TPD, TPD), all_blocks)
     flat_tiles = three_center.reshape(aux_rows, ntiles * area)
     piece = lax.all_gather(kernel, "pair", axis=0, tiled=True)

time: 244 us -> 262 us (1.074)
  waiting for transfers between devices: 184 us -> 202 us
  blocking collectives: 17.9 us -> 0 us
  starting transfers between devices: 0.04 us -> 16.8 us
    all_gather x1 -> x0, blocking collectives: 17.9 us -> none  [shards(): all_blocks = lax.all_gather(own_blocks, 'pair', axis=0, tiled=True)]
    ppermute x0 -> x15, starting transfers between devices: none -> 16.7 us  [the longest x7 16.4 us: shards(): lax.ppermute(going_down, 'pair', [(d, (d - 1) % ways) for d in range(ways)])]
    ppermute x0 -> x15, waiting for transfers between devices: none -> 11.6 us  [the longest x8 10.3 us: shards(): lax.ppermute(going_up, 'pair', [(d, (d + 1) % ways) for d in range(ways)])]
    all_gather x1, waiting for transfers between devices: 103 us -> 110 us  [shards(): piece = lax.all_gather(kernel, 'pair', axis=0, tiled=True)]
    unnamed x8 -> x11, local copies, waits for them, and re-layouts: 5.55 us -> 4.82 us
  transfers between devices with their start and end apart: 2 -> 17, of which waited for: 2 -> 15; matrix products, arithmetic and copies ran while one was open for 0% -> 3% of each run, Pallas kernels for 0% -> 0%
where the time goes in v1:
time: 262 us
  waiting for transfers between devices  202 us (77%)
  matrix products  18.9 us (7%)
  starting transfers between devices  16.8 us (6%)
  between operations  13.5 us (5%)
  local copies, waits for them, and re-layouts  10.4 us (4%)
    all_gather x1, waiting for transfers between devices, shards(): piece = lax.all_gather(kernel, 'pair', axis=0, tiled=True)  110 us
    unnamed x3, waiting for transfers between devices  80.7 us
    ppermute x7, starting transfers between devices, shards(): lax.ppermute(going_down, 'pair', [(d, (d - 1) % ways) for d in range(ways)])  16.4 us
    ppermute x8, waiting for transfers between devices, shards(): lax.ppermute(going_up, 'pair', [(d, (d + 1) % ways) for d in range(ways)])  10.3 us
    dot_general x1, matrix products, shards(): lax.dot_general(flat_tiles, flat_piece, (((1,), (1,)), ((), ())), preferr...  9.48 us
  transfers between devices with their start and end apart: 17, of which 15 were waited for; matrix products, arithmetic and copies ran while one was open for 3% of the time, Pallas kernels for 0%

profile of v1, /device:TPU:32, one launch (start us, length us, event | category | flops | bytes accessed | tf_op | source)
XLA Modules:
  0.0 261.8 jit_solution(7450951956108083363)
XLA Ops:
  6.6 1.7 collective-permute-start.1
  8.3 1.1 convolution_convert_fusion
  9.4 1.7 reshape.46
  11.1 1.2 copy.14
  12.3 4.4 %fusion.7 = bf16[144,16,16,16]{0,2,3,1:T(8,128)(2,1)} fusion(bf16[144,16,16,16]{0,3,2,1:T(8,128)(2,1)S(1)} %bitcast.43, bf16[16,16,16,16,1]{3,2,1,0,4:T(8,128)(2,1)} %reshape.46), kind=kOutput, calls=%fused_computation.7 | convolution fusion | flops 302579712 | bytes 2490368 | tf_op jit(solution)/shard_map/tkml,pkln->ptmn/dot_general | solution.py:27
  17.0 1.5 collective-permute-start.3
  18.5 1.2 collective-permute-done.2
  19.8 1.7 collective-permute-start.5
  21.5 1.2 collective-permute-done.4
  22.8 2.8 %collective-permute-start.7 = (bf16[2,256]{1,0:T(2,128)(2,1)S(1)}, bf16[2,256]{1,0:T(2,128)(2,1)S(1)}, u32[]{:S(2)}, u32[]{:S(2)}) collective-permute-start(bf16[2,256]{1,0:T(2,128)(2,1)S(1)} %collective-permute-done.5), channel_id=1, source_target_pairs={{0,240},{16,0},{32,16},{48,32},{64,48},{80,64},{96,80},{112,96},{1... | collective-permute-start | bytes 3080 | tf_op jit(solution)/shard_map/ppermute | solution.py:60
  25.6 1.0 collective-permute-done.6
  26.9 2.9 %collective-permute-start.9 = (bf16[2,256]{1,0:T(2,128)(2,1)S(1)}, bf16[2,256]{1,0:T(2,128)(2,1)S(1)}, u32[]{:S(2)}, u32[]{:S(2)}) collective-permute-start(bf16[2,256]{1,0:T(2,128)(2,1)S(1)} %collective-permute-done.7), channel_id=1, source_target_pairs={{0,240},{16,0},{32,16},{48,32},{64,48},{80,64},{96,80},{112,96},{1... | collective-permute-start | bytes 3080 | tf_op jit(solution)/shard_map/ppermute | solution.py:60
  29.8 1.0 collective-permute-done.8
  31.1 2.9 %collective-permute-start.11 = (bf16[2,256]{1,0:T(2,128)(2,1)S(1)}, bf16[2,256]{1,0:T(2,128)(2,1)S(1)}, u32[]{:S(2)}, u32[]{:S(2)}) collective-permute-start(bf16[2,256]{1,0:T(2,128)(2,1)S(1)} %collective-permute-done.9), channel_id=1, source_target_pairs={{0,240},{16,0},{32,16},{48,32},{64,48},{80,64},{96,80},{112,96},{1... | collective-permute-start | bytes 3080 | tf_op jit(solution)/shard_map/ppermute | solution.py:60
  35.3 2.9 %collective-permute-start.13 = (bf16[2,256]{1,0:T(2,128)(2,1)S(1)}, bf16[2,256]{1,0:T(2,128)(2,1)S(1)}, u32[]{:S(2)}, u32[]{:S(2)}) collective-permute-start(bf16[2,256]{1,0:T(2,128)(2,1)S(1)} %collective-permute-done.11), channel_id=1, source_target_pairs={{0,240},{16,0},{32,16},{48,32},{64,48},{80,64},{96,80},{112,96},{1... | collective-permute-start | bytes 3080 | tf_op jit(solution)/shard_map/ppermute | solution.py:60
  38.2 1.0 collective-permute-done.12
  39.5 3.9 %collective-permute-done.14 = bf16[2,256]{1,0:T(2,128)(2,1)S(1)} collective-permute-done((bf16[2,256]{1,0:T(2,128)(2,1)S(1)}, bf16[2,256]{1,0:T(2,128)(2,1)S(1)}, u32[]{:S(2)}, u32[]{:S(2)}) %collective-permute-start.14) | collective-permute-done | bytes 1056 | tf_op jit(solution)/shard_map/ppermute | solution.py:57
  43.7 3.7 %fusion.4 = bf16[16,16,144,16]{2,1,3,0:T(8,128)(2,1)} fusion(bf16[144,16,16,16]{0,2,3,1:T(8,128)(2,1)} %fusion.7, bf16[16,16,16]{2,1,0:T(8,128)(2,1)S(1)} %reshape.42), kind=kOutput, calls=%fused_computation.6 | convolution fusion | flops 19464192 | bytes 2367488 | tf_op jit(solution)/shard_map/pojml,oijln->poimn/dot_general | solution.py:41
  47.5 3.6 %copy.18 = bf16[144,16,256]{2,0,1:T(8,128)(2,1)} copy(bf16[144,16,256]{0,2,1:T(8,128)(2,1)} %bitcast.44) | data formatting | bytes 2359296 | tf_op jit(solution)/shard_map/convert_element_type | solution.py:42
  51.2 110.0 %all-gather.2.cloned.1.call-done = bf16[2304,16,256]{2,0,1:T(8,128)(2,1)} async-done(((bf16[144,16,256]{2,0,1:T(8,128)(2,1)}), bf16[2304,16,256]{2,0,1:T(8,128)(2,1)}) %all-gather.2.cloned.1.call-update) | async-done | bytes 18874384 | tf_op jit(solution)/shard_map/all_gather | solution.py:69
  161.2 9.5 %convolution_bitcast_fusion = f32[144,2304]{1,0:T(8,128)S(1)} fusion(bf16[2304,16,256]{2,0,1:T(8,128)(2,1)} %all-gather.2.cloned.1.call-done, bf16[144,16,256]{0,2,1:T(8,128)(2,1)S(1)} %copy.14), kind=kOutput, calls=%fused_computation.1 | convolution fusion | flops 2717908992 | bytes 21381120 | tf_op jit(solution)/shard_map/dot_general | solution.py:71
  170.7 1.9 copy.25
  172.6 80.7 %reduce-scatter.4.cloned.1.call-done = f32[144,144]{1,0:T(8,128)} async-done(((f32[2304,144]{1,0:T(8,128)}), f32[144,144]{1,0:T(8,128)}) %reduce-scatter.4.cloned.1.call-update) | async-done | bytes 82960
  253.3 1.7 copy.26
  (48 shorter events, 3.1 us)
Async XLA Ops:
  6.5 1.8 copy-start
  6.5 4.5 %copy-start.1 = (bf16[144,16,256]{2,1,0:T(8,128)(2,1)S(1)}, bf16[144,16,256]{2,1,0:T(8,128)(2,1)}, u32[]{:S(2)}) copy-start(bf16[144,16,256]{2,1,0:T(8,128)(2,1)} %param.6) | copy-start | bytes 3538948
  6.5 154.6 %all-gather.2.cloned.1.call-start = ((), (), s32[]{:S(2)}) async-start(), calls=%async_computation.1 | async-start | bytes 20054016 | tf_op jit(solution)/shard_map/all_gather | solution.py:69
  6.5 10.2 %collective-permute-start = (bf16[2,256]{1,0:T(2,128)(2,1)}, bf16[2,256]{1,0:T(2,128)(2,1)S(1)}, u32[]{:S(2)}, u32[]{:S(2)}) collective-permute-start(bf16[2,256]{1,0:T(2,128)(2,1)} %bitcast.46), channel_id=1, source_target_pairs={{0,16},{16,32},{32,48},{48,64},{64,80},{80,96},{96,112},{112,128},... | collective-permute-start | bytes 3080 | tf_op jit(solution)/shard_map/ppermute | solution.py:57
  6.6 10.5 %collective-permute-start.1 = (bf16[2,256]{1,0:T(2,128)(2,1)}, bf16[2,256]{1,0:T(2,128)(2,1)S(1)}, u32[]{:S(2)}, u32[]{:S(2)}) collective-permute-start(bf16[2,256]{1,0:T(2,128)(2,1)} %bitcast.47), channel_id=1, source_target_pairs={{0,240},{16,0},{32,16},{48,32},{64,48},{80,64},{96,80},{112,96},{1... | collective-permute-start | bytes 3080 | tf_op jit(solution)/shard_map/ppermute | solution.py:60
  9.4 2.9 %copy-start.2 = (bf16[1,2,256]{2,1,0:T(2,128)(2,1)S(1)}, bf16[1,2,256]{2,1,0:T(2,128)(2,1)}, u32[]{:S(2)}) copy-start(bf16[1,2,256]{2,1,0:T(2,128)(2,1)} %param.11) | copy-start | bytes 3076
  12.3 31.1 %copy-start.3 = (s32[1,16,1]{1,2,0:T(1,128)S(1)}, s32[1,16,1]{1,2,0:T(1,128)}, u32[]{:S(2)}) copy-start(s32[1,16,1]{1,2,0:T(1,128)} %param.10) | copy-start | bytes 196
  16.7 3.0 %collective-permute-start.2 = (bf16[2,256]{1,0:T(2,128)(2,1)S(1)}, bf16[2,256]{1,0:T(2,128)(2,1)S(1)}, u32[]{:S(2)}, u32[]{:S(2)}) collective-permute-start(bf16[2,256]{1,0:T(2,128)(2,1)S(1)} %collective-permute-done), channel_id=1, source_target_pairs={{0,16},{16,32},{32,48},{48,64},{64,80},{80,96},{96,112},{112,128},... | collective-permute-start | bytes 3080 | tf_op jit(solution)/shard_map/ppermute | solution.py:57
  17.0 2.8 %collective-permute-start.3 = (bf16[2,256]{1,0:T(2,128)(2,1)S(1)}, bf16[2,256]{1,0:T(2,128)(2,1)S(1)}, u32[]{:S(2)}, u32[]{:S(2)}) collective-permute-start(bf16[2,256]{1,0:T(2,128)(2,1)S(1)} %collective-permute-done.1), channel_id=1, source_target_pairs={{0,240},{16,0},{32,16},{48,32},{64,48},{80,64},{96,80},{112,96},{1... | collective-permute-start | bytes 3080 | tf_op jit(solution)/shard_map/ppermute | solution.py:60
  19.7 3.0 %collective-permute-start.4 = (bf16[2,256]{1,0:T(2,128)(2,1)S(1)}, bf16[2,256]{1,0:T(2,128)(2,1)S(1)}, u32[]{:S(2)}, u32[]{:S(2)}) collective-permute-start(bf16[2,256]{1,0:T(2,128)(2,1)S(1)} %collective-permute-done.2), channel_id=1, source_target_pairs={{0,16},{16,32},{32,48},{48,64},{64,80},{80,96},{96,112},{112,128},... | collective-permute-start | bytes 3080 | tf_op jit(solution)/shard_map/ppermute | solution.py:57
  19.8 3.0 %collective-permute-start.5 = (bf16[2,256]{1,0:T(2,128)(2,1)S(1)}, bf16[2,256]{1,0:T(2,128)(2,1)S(1)}, u32[]{:S(2)}, u32[]{:S(2)}) collective-permute-start(bf16[2,256]{1,0:T(2,128)(2,1)S(1)} %collective-permute-done.3), channel_id=1, source_target_pairs={{0,240},{16,0},{32,16},{48,32},{64,48},{80,64},{96,80},{112,96},{1... | collective-permute-start | bytes 3080 | tf_op jit(solution)/shard_map/ppermute | solution.py:60
  22.7 3.9 %collective-permute-start.6 = (bf16[2,256]{1,0:T(2,128)(2,1)S(1)}, bf16[2,256]{1,0:T(2,128)(2,1)S(1)}, u32[]{:S(2)}, u32[]{:S(2)}) collective-permute-start(bf16[2,256]{1,0:T(2,128)(2,1)S(1)} %collective-permute-done.4), channel_id=1, source_target_pairs={{0,16},{16,32},{32,48},{48,64},{64,80},{80,96},{96,112},{112,128},... | collective-permute-start | bytes 3080 | tf_op jit(solution)/shard_map/ppermute | solution.py:57
  22.8 4.1 %collective-permute-start.7 = (bf16[2,256]{1,0:T(2,128)(2,1)S(1)}, bf16[2,256]{1,0:T(2,128)(2,1)S(1)}, u32[]{:S(2)}, u32[]{:S(2)}) collective-permute-start(bf16[2,256]{1,0:T(2,128)(2,1)S(1)} %collective-permute-done.5), channel_id=1, source_target_pairs={{0,240},{16,0},{32,16},{48,32},{64,48},{80,64},{96,80},{112,96},{1... | collective-permute-start | bytes 3080 | tf_op jit(solution)/shard_map/ppermute | solution.py:60
  26.6 4.2 %collective-permute-start.8 = (bf16[2,256]{1,0:T(2,128)(2,1)S(1)}, bf16[2,256]{1,0:T(2,128)(2,1)S(1)}, u32[]{:S(2)}, u32[]{:S(2)}) collective-permute-start(bf16[2,256]{1,0:T(2,128)(2,1)S(1)} %collective-permute-done.6), channel_id=1, source_target_pairs={{0,16},{16,32},{32,48},{48,64},{64,80},{80,96},{96,112},{112,128},... | collective-permute-start | bytes 3080 | tf_op jit(solution)/shard_map/ppermute | solution.py:57
  26.9 4.2 %collective-permute-start.9 = (bf16[2,256]{1,0:T(2,128)(2,1)S(1)}, bf16[2,256]{1,0:T(2,128)(2,1)S(1)}, u32[]{:S(2)}, u32[]{:S(2)}) collective-permute-start(bf16[2,256]{1,0:T(2,128)(2,1)S(1)} %collective-permute-done.7), channel_id=1, source_target_pairs={{0,240},{16,0},{32,16},{48,32},{64,48},{80,64},{96,80},{112,96},{1... | collective-permute-start | bytes 3080 | tf_op jit(solution)/shard_map/ppermute | solution.py:60
  30.8 4.2 %collective-permute-start.10 = (bf16[2,256]{1,0:T(2,128)(2,1)S(1)}, bf16[2,256]{1,0:T(2,128)(2,1)S(1)}, u32[]{:S(2)}, u32[]{:S(2)}) collective-permute-start(bf16[2,256]{1,0:T(2,128)(2,1)S(1)} %collective-permute-done.8), channel_id=1, source_target_pairs={{0,16},{16,32},{32,48},{48,64},{64,80},{80,96},{96,112},{112,128},... | collective-permute-start | bytes 3080 | tf_op jit(solution)/shard_map/ppermute | solution.py:57
  31.1 4.2 %collective-permute-start.11 = (bf16[2,256]{1,0:T(2,128)(2,1)S(1)}, bf16[2,256]{1,0:T(2,128)(2,1)S(1)}, u32[]{:S(2)}, u32[]{:S(2)}) collective-permute-start(bf16[2,256]{1,0:T(2,128)(2,1)S(1)} %collective-permute-done.9), channel_id=1, source_target_pairs={{0,240},{16,0},{32,16},{48,32},{64,48},{80,64},{96,80},{112,96},{1... | collective-permute-start | bytes 3080 | tf_op jit(solution)/shard_map/ppermute | solution.py:60
  35.0 4.2 %collective-permute-start.12 = (bf16[2,256]{1,0:T(2,128)(2,1)S(1)}, bf16[2,256]{1,0:T(2,128)(2,1)S(1)}, u32[]{:S(2)}, u32[]{:S(2)}) collective-permute-start(bf16[2,256]{1,0:T(2,128)(2,1)S(1)} %collective-permute-done.10), channel_id=1, source_target_pairs={{0,16},{16,32},{32,48},{48,64},{64,80},{80,96},{96,112},{112,128},... | collective-permute-start | bytes 3080 | tf_op jit(solution)/shard_map/ppermute | solution.py:57
  35.3 4.2 %collective-permute-start.13 = (bf16[2,256]{1,0:T(2,128)(2,1)S(1)}, bf16[2,256]{1,0:T(2,128)(2,1)S(1)}, u32[]{:S(2)}, u32[]{:S(2)}) collective-permute-start(bf16[2,256]{1,0:T(2,128)(2,1)S(1)} %collective-permute-done.11), channel_id=1, source_target_pairs={{0,240},{16,0},{32,16},{48,32},{64,48},{80,64},{96,80},{112,96},{1... | collective-permute-start | bytes 3080 | tf_op jit(solution)/shard_map/ppermute | solution.py:60
  39.2 4.2 %collective-permute-start.14 = (bf16[2,256]{1,0:T(2,128)(2,1)S(1)}, bf16[2,256]{1,0:T(2,128)(2,1)S(1)}, u32[]{:S(2)}, u32[]{:S(2)}) collective-permute-start(bf16[2,256]{1,0:T(2,128)(2,1)S(1)} %collective-permute-done.12), channel_id=1, source_target_pairs={{0,16},{16,32},{32,48},{48,64},{64,80},{80,96},{96,112},{112,128},... | collective-permute-start | bytes 3080 | tf_op jit(solution)/shard_map/ppermute | solution.py:57
  51.1 202.2 %reduce-scatter.4.cloned.1.call-start = ((), (), s32[]{:S(2)}) async-start(), calls=%async_computation.2 | async-start | bytes 2506752
Sparse Core Ops, SparseCore 0:
  51.3 109.8 all-gather.1
  172.7 80.5 reduce-scatter.3
